TPU v7x, 32 devices: a whole 2x2x4 slice. The times are simulated.
32 devices in a mesh: req: 4 (over y, core), seq: 8 (over z, x).
Axes of the slice: x: 2, y: 2, z: 4, core: 2. Of those that a mesh axis runs over, the one named last changes fastest.
Arguments:
- latent_cache: bfloat16 [4, 4096, 576], P('req', 'seq'), may hold values from -16 to 16
- queries: bfloat16 [4, 3, 128, 576], P('req', None, 'seq'), may hold values from -16 to 16
- chosen: int32 [4, 3, 32], P('req'), may hold values from 0 to 63, as said below
- position: int32 [4], P('req'), may hold values from 4033 to 4096
- w_value: bfloat16 [128, 512, 128], P('seq'), may hold values from -1.5 to 1.5
- w_out: bfloat16 [16384, 7168], P('seq', 'req'), may hold values from -0.0625 to 0.0625
Outputs:
- mixed_out: bfloat16 [7168, 12], P(('req', 'seq'))
Inputs may be any that keep to these rules, and one draw needn't show every extreme that they name: `chosen`: block b holds positions b * 64 to b * 64 + 63, which lie on shard b // 8 of seq. A query's 32 numbers are distinct; at most 8 of them lie on one shard and exactly 8 on some shard, for every query; every query names the last block; its blocks on the other shards are spread as evenly as possible over those shards.
All inputs are finite; a program needn't handle non-finite values.
Results may differ from a plain program's by a relative error of at most 0.013.
Values may be sent and summed in bfloat16 or wider, within the bound.
A program may use at most 128 MiB of HBM per device.

v0:
```python
import math

import jax
import jax.numpy as jnp
from jax import lax
from jax.sharding import PartitionSpec as P

LATENT = 512
BLOCK = 64
MAXB = 8


score_scale = 1.0 / math.sqrt(192.0)
very_low = -1e30


def joined(value, axis, join):
    pieces = jax.tree.map(lambda part: lax.all_gather(part, axis), value)
    head = jax.tree.map(lambda part: part[0], pieces)
    tail = jax.tree.map(lambda part: part[1:], pieces)
    running, _ = lax.scan(lambda running, section: (join(running, section), None), head, tail)
    return running


def join_parts(left_part, right_part):
    peak_left, total_left, summed_left = left_part
    peak_right, total_right, summed_right = right_part
    peak_new = jnp.maximum(peak_left, peak_right)
    factor_left = jnp.exp(peak_left - peak_new)
    factor_right = jnp.exp(peak_right - peak_new)
    total_new = total_left * factor_left + total_right * factor_right
    summed_new = summed_left * factor_left[:, :, None] + summed_right * factor_right[:, :, None]
    return (peak_new, total_new, summed_new)


def local_blocks(chosen_rows, shard_index, per_shard):
    owned_here = (chosen_rows // per_shard == shard_index).astype(jnp.int32)
    ranked = jnp.cumsum(owned_here, axis=1) - 1
    target = jnp.arange(MAXB, dtype=jnp.int32)
    matched = (owned_here[:, :, None] == 1) & (ranked[:, :, None] == target[None, None, :])
    offset = jnp.sum(jnp.where(matched, (chosen_rows % per_shard)[:, :, None], 0), axis=1)
    return (offset, jnp.any(matched, axis=1))


def body(latent_cache, queries, chosen, position, w_value, w_out):
    req_dev, cache_len, key_width = latent_cache.shape
    step_count = queries.shape[1]
    query_count = req_dev * step_count
    per_shard = cache_len // BLOCK
    shard_index = lax.axis_index("seq")
    all_heads = lax.all_gather(queries, "seq", axis=2, tiled=True)
    query_rows = all_heads.reshape(query_count, all_heads.shape[2], key_width)
    offset, filled = local_blocks(
        chosen.reshape(query_count, chosen.shape[2]), shard_index, per_shard
    )
    request_of = jnp.arange(query_count, dtype=jnp.int32) // step_count
    inside = jnp.arange(BLOCK, dtype=jnp.int32)
    local_row = offset[:, :, None] * BLOCK + inside[None, None, :]
    flat_rows = (request_of[:, None, None] * cache_len + local_row).reshape(query_count, -1)
    gathered = jnp.take(latent_cache.reshape(req_dev * cache_len, key_width), flat_rows, axis=0)
    position_limit = jnp.broadcast_to(position[:, None], (req_dev, step_count)).reshape(-1)
    usable = filled[:, :, None] & (
        shard_index * cache_len + local_row < position_limit[:, None, None]
    )
    usable = usable.reshape(query_count, -1)
    scores = (
        jnp.einsum("qhk,qnk->qhn", query_rows, gathered, preferred_element_type=jnp.float32)
        * score_scale
    )
    scores = jnp.where(usable[:, None, :], scores, very_low)
    row_peak = jnp.max(scores, axis=2)
    raw_weights = jnp.where(usable[:, None, :], jnp.exp(scores - row_peak[:, :, None]), 0.0)
    row_total = jnp.sum(raw_weights, axis=2)
    latent_part = lax.slice_in_dim(gathered, 0, LATENT, axis=2)
    weighted = jnp.einsum(
        "qhn,qnl->qhl",
        raw_weights.astype(jnp.bfloat16),
        latent_part,
        preferred_element_type=jnp.float32,
    )
    heads_dev = w_value.shape[0]
    peak_all, total_all, weighted_all = joined((row_peak, row_total, weighted), "seq", join_parts)
    first_head = shard_index * heads_dev
    total_mine = lax.dynamic_slice_in_dim(total_all, first_head, heads_dev, 1)
    weighted_mine = lax.dynamic_slice_in_dim(weighted_all, first_head, heads_dev, 1)
    latent_out = (weighted_mine / total_mine[:, :, None]).astype(jnp.bfloat16)
    head_out = jnp.einsum(
        "qhl,hlv->qhv", latent_out, w_value, preferred_element_type=jnp.float32
    ).astype(jnp.bfloat16)
    head_out = head_out.reshape(req_dev, step_count, heads_dev * w_value.shape[2])
    every_request = lax.all_gather(head_out, "req", axis=0, tiled=True)
    flat_heads = every_request.reshape(-1, every_request.shape[2])
    mixed_out = lax.psum_scatter(
        lax.dot_general(
            w_out, flat_heads, (((0,), (1,)), ((), ())), preferred_element_type=jnp.float32
        ),
        "seq",
        scatter_dimension=0,
        tiled=True,
    )
    return mixed_out.astype(jnp.bfloat16)


def solution(mesh):
    return jax.shard_map(
        body,
        mesh=mesh,
        in_specs=(
            P("req", "seq", None),
            P("req", None, "seq", None),
            P("req", None, None),
            P("req"),
            P("seq", None, None),
            P("seq", "req"),
        ),
        out_specs=P(("req", "seq"), None),
        check_vma=False,
    )
```

profile of v0, /device:TPU:0, one launch (start us, length us, event | category | flops | bytes accessed | tf_op | source)
XLA Modules:
  0.0 252.5 jit_solution(506263668769754829)
XLA Ops:
  6.5 0.0 copy-start
  6.5 0.0 all-gather.7.cloned.1.call-start
  6.5 0.8 broadcast_compare_fusion.1
  7.4 0.2 reduce_window_sum.11
  7.6 0.7 add_select_fusion
  8.3 0.1 fusion.17
  8.4 0.2 select_reduce_fusion
  8.6 0.1 add.142
  8.7 0.1 add.154
  8.7 0.1 add.143
  9.5 0.1 and.76
  9.6 0.1 and.77
  9.7 0.1 add.145
  9.7 0.1 compare_select_fusion
  9.8 33.2 %all_gather.24 = bf16[1,3,128,576]{3,2,1,0:T(8,128)(2,1)S(1)} all-gather(bf16[1,3,16,576]{3,2,1,0:T(8,128)(2,1)} %param.9), channel_id=1, replica_groups=mesh['req'=4,'seq'=8] {'seq'}, dimensions={2}, use_global_device_ids=true | all-gather | bytes 497664 | tf_op jit(solution)/shard_map/all_gather | solution.py:51
  43.0 1.4 copy.22
  44.4 5.6 %gather_fusion = bf16[1536,576]{1,0:T(8,128)(2,1)} fusion(bf16[512,576]{1,0:T(8,128)(2,1)S(1)} %bitcast.76, s32[2048]{0:T(1024)S(1)} %pad_clamp_fusion), kind=kCustom, calls=%fused_computation | custom fusion | bytes 3545088 | tf_op jit(solution)/shard_map/jit(_take)/gather | solution.py:60
  49.9 0.1 fusion.18
  50.0 1.9 broadcast_select_fusion
  51.9 0.7 fusion.27
  52.6 1.6 fusion.3
  54.2 0.0 all-gather.7.cloned.1.call-update
  54.2 0.0 reduce-scatter.4.cloned.1.call-start
  54.3 26.9 %all-gather.3 = f32[8,3,128]{2,1,0:T(4,128)S(1)} all-gather(f32[1,3,128]{2,1,0:T(4,128)S(1)} %bitcast.79), channel_id=2, replica_groups=mesh['req'=4,'seq'=8] {'seq'}, dimensions={0}, use_global_device_ids=true | all-gather | bytes 13824 | tf_op jit(solution)/shard_map/all_gather | solution.py:18
  81.2 0.3 fusion.9
  81.5 27.0 %all-gather.4 = f32[8,3,128]{2,1,0:T(4,128)S(1)} all-gather(f32[1,3,128]{2,1,0:T(4,128)S(1)} %bitcast.80), channel_id=3, replica_groups=mesh['req'=4,'seq'=8] {'seq'}, dimensions={0}, use_global_device_ids=true | all-gather | bytes 13824 | tf_op jit(solution)/shard_map/all_gather | solution.py:18
  108.5 46.0 %all-gather.7.cloned.1.call-done = f32[24,128,512]{2,1,0:T(8,128)} async-done(((f32[3,128,512]{2,1,0:T(8,128)}), f32[24,128,512]{2,1,0:T(8,128)}) %all-gather.7.cloned.1.call-update) | async-done | bytes 6291472 | tf_op jit(solution)/shard_map/all_gather | solution.py:18
  154.5 0.0 slice-start
  154.5 6.0 %slice.46 = f32[21,128,512]{2,1,0:T(8,128)} slice(f32[24,128,512]{2,1,0:T(8,128)} %all-gather.7.cloned.1.call-done), slice={[3:24], [0:128], [0:512]} | slice | bytes 11010048 | tf_op jit(solution)/shard_map/slice | solution.py:20
  160.6 0.0 slice-done
  160.6 9.9 %while.14 = (s32[]{:T(128)}, f32[3,128]{1,0:T(4,128)S(1)}, f32[3,128]{1,0:T(4,128)S(1)}, f32[3,128,512]{2,1,0:T(8,128)S(1)}, f32[7,3,128]{2,1,0:T(4,128)S(1)}, /...) while((s32[]{:T(128)}, f32[3,128]{1,0:T(4,128)S(1)}, f32[3,128]{1,0:T(4,128)S(1)}, ...), condition=%wide.region_6.7_spmd, body=%wide.region_5.6_spmd.sunk | while | flops 592130 | bytes 2374757 | solution.py:21
  160.6 1.4 fusion.35
  162.0 1.4 fusion.35
  163.4 1.4 fusion.35
  164.8 1.4 fusion.35
  166.2 1.4 fusion.35
  167.7 1.4 fusion.35
  169.1 1.4 fusion.35
  170.4 0.1 constant_dynamic-slice_fusion
  170.5 0.1 divide_convert_fusion
  170.6 0.0 copy-done
  170.6 0.4 fusion.7
  171.0 5.2 %all_gather.31 = bf16[4,3,2048]{2,1,0:T(4,128)(2,1)S(1)} all-gather(bf16[1,3,2048]{2,1,0:T(4,128)(2,1)S(1)} %fusion.7), channel_id=1, replica_groups=mesh['req'=4,'seq'=8] {'req'}, dimensions={0}, use_global_device_ids=true | all-gather | bytes 61440 | tf_op jit(solution)/shard_map/all_gather | solution.py:91
  176.3 4.1 %convolution_bitcast_fusion = f32[1792,12]{0,1:T(8,128)S(1)} fusion(bf16[12,2048]{1,0:T(8,128)(2,1)S(1)} %reshape.254, bf16[2048,1792]{1,0:T(8,128)(2,1)} %param.13), kind=kOutput, calls=%fused_computation.9 | convolution fusion | flops 88080384 | bytes 7475200 | tf_op jit(solution)/shard_map/dot_general | solution.py:94
  180.4 1.3 copy.29
  181.7 0.0 reduce-scatter.4.cloned.1.call-update
  181.7 62.3 %reduce-scatter.4.cloned.1.call-done = f32[224,12]{1,0:T(8,128)} async-done(((f32[1792,12]{1,0:T(8,128)}), f32[224,12]{1,0:T(8,128)}) %reduce-scatter.4.cloned.1.call-update) | async-done | bytes 10768
  244.1 1.6 copy.30
  (17 shorter events, 0.3 us)
Async XLA Ops:
  6.5 164.1 %copy-start = (bf16[16,512,128]{2,1,0:T(8,128)(2,1)S(1)}, bf16[16,512,128]{2,1,0:T(8,128)(2,1)}, u32[]{:S(2)}) copy-start(bf16[16,512,128]{2,1,0:T(8,128)(2,1)} %param.12) | copy-start | bytes 6291460
  6.5 148.0 %all-gather.7.cloned.1.call-start = ((), (), s32[]{:S(2)}) async-start(), calls=%async_computation.1 | async-start | bytes 7077888 | tf_op jit(solution)/shard_map/all_gather | solution.py:18
  54.2 189.8 %reduce-scatter.4.cloned.1.call-start = ((), (), s32[]{:S(2)}) async-start(), calls=%async_computation.2 | async-start | bytes 1032192
  154.5 6.0 %slice-start = ((f32[24,128,512]{2,1,0:T(8,128)}), f32[3,128,512]{2,1,0:T(8,128)S(1)}, s32[]{:S(2)}) async-start(f32[24,128,512]{2,1,0:T(8,128)} %all-gather.7.cloned.1.call-done), calls=%async_computation.3 | async-start | bytes 1572864 | tf_op jit(solution)/shard_map/slice | solution.py:19
Sparse Core Ops, SparseCore 0:
  54.3 100.1 all-gather.6
  181.8 62.1 reduce-scatter.3
where the time goes:
time: 253 us; the launch traced here: 252 us
  waiting for transfers between devices  108 us (43%)
  blocking collectives  92.3 us (36%)
  local copies, waits for them, and re-layouts  16.4 us (6%)
  other arithmetic  14.2 us (6%)
  between operations  14.1 us (6%)
  matrix products  6.84 us (3%)
    unnamed x3, waiting for transfers between devices  62.4 us
    all_gather x2, blocking collectives, joined(): pieces = jax.tree.map(lambda part: lax.all_gather(part, axis), value)  53.9 us
    all_gather x1, waiting for transfers between devices, joined(): pieces = jax.tree.map(lambda part: lax.all_gather(part, axis), value)  46 us
    all_gather x1, blocking collectives, body(): all_heads = lax.all_gather(queries, 'seq', axis=2, tiled=True)  33.2 us
    add x7, other arithmetic, join_parts(): summed_left * factor_left[:, :, None]  9.56 us
    slice x3, local copies, waits for them, and re-layouts, joined(): tail = jax.tree.map(lambda part: part[1:], pieces)  6.05 us
    gather x1, local copies, waits for them, and re-layouts, body(): jnp.take(latent_cache.reshape(req_dev * cache_len, key_width), flat_rows,...  5.55 us
    all_gather x1, blocking collectives, body(): every_request = lax.all_gather(head_out, 'req', axis=0, tiled=True)  5.23 us
  transfers between devices with their start and end apart: 2, of which 2 were waited for; matrix products, arithmetic and copies ran while one was open for 0% of the time, Pallas kernels for 0%

commit v1 on v0

v1 whole, which is shorter than its diff:
```python
import functools
import math

import jax
import jax.numpy as jnp
from jax import lax
from jax.experimental import pallas as pl
from jax.experimental.pallas import tpu as pltpu
from jax.sharding import PartitionSpec as P

LATENT = 512
BLOCK = 64
LANES = 128
STATS = 128
MESH = pl.DeviceIdType.MESH

score_scale = 1.0 / math.sqrt(192.0)
very_low = -1e30


def kernel(
    n_seq, n_req, steps, heads,
    chosen_ref, position_ref, q_hbm, cache_hbm, wv_hbm, wo_hbm,
    out_ref,
    qbuf, cache, wv, wo, mask, part, got, lat, hf, hsend, hall, hwide, ysend, yrecv,
    load_sem, q_send, q_recv, p_send, p_recv, h_send, h_recv, y_send, y_recv,
):
    me = lax.axis_index("seq")
    req = lax.axis_index("req")
    rows = steps * heads
    cache_len = cache.shape[0]
    cols = ysend.shape[2]

    loads = [
        pltpu.make_async_copy(q_hbm, qbuf.at[0], load_sem.at[0]),
        pltpu.make_async_copy(cache_hbm, cache, load_sem.at[1]),
        pltpu.make_async_copy(wv_hbm, wv, load_sem.at[2]),
        pltpu.make_async_copy(wo_hbm, wo, load_sem.at[3]),
    ]
    loads[0].start()
    loads[1].start()

    def seq_at(offset):
        return {"seq": lax.rem(me + offset + n_seq, n_seq)}

    def req_at(offset):
        return {"req": lax.rem(req + offset + n_req, n_req)}

    barrier = pltpu.get_barrier_semaphore()
    for d in range(1, n_seq):
        pl.semaphore_signal(barrier, inc=1, device_id=seq_at(d), device_id_type=MESH)
    for e in range(1, n_req):
        pl.semaphore_signal(barrier, inc=1, device_id=req_at(e), device_id_type=MESH)
    pl.semaphore_wait(barrier, n_seq + n_req - 2)

    def query_copy(d):
        return pltpu.make_async_remote_copy(
            src_ref=q_hbm, dst_ref=qbuf.at[d], send_sem=q_send.at[d], recv_sem=q_recv.at[d],
            device_id=seq_at(d), device_id_type=MESH,
        )

    def part_copy(d):
        return pltpu.make_async_remote_copy(
            src_ref=part.at[d], dst_ref=got.at[d], send_sem=p_send.at[d], recv_sem=p_recv.at[d],
            device_id=seq_at(-d), device_id_type=MESH,
        )

    def head_copy(e):
        return pltpu.make_async_remote_copy(
            src_ref=hsend, dst_ref=hall.at[req], send_sem=h_send.at[e], recv_sem=h_recv.at[e],
            device_id=req_at(e), device_id_type=MESH,
        )

    def out_copy(d):
        return pltpu.make_async_remote_copy(
            src_ref=ysend.at[lax.rem(me + d, n_seq)], dst_ref=yrecv.at[d],
            send_sem=y_send.at[d], recv_sem=y_recv.at[d],
            device_id=seq_at(d), device_id_type=MESH,
        )

    order = sorted(range(1, n_seq), key=lambda d: (min(d, n_seq - d), d))
    for d in order:
        query_copy(d).start()
    loads[2].start()
    loads[3].start()

    block = me * (cache_len // BLOCK) + lax.broadcasted_iota(jnp.int32, (1, cache_len), 1) // BLOCK
    inside = me * cache_len + lax.broadcasted_iota(jnp.int32, (1, cache_len), 1) < position_ref[0]
    row_step = lax.broadcasted_iota(jnp.int32, (rows, cache_len), 0) // heads
    usable = jnp.zeros((rows, cache_len), jnp.float32)
    for t in range(steps):
        named = block == chosen_ref[t, 0]
        for k in range(1, chosen_ref.shape[1]):
            named = named | (block == chosen_ref[t, k])
        flag = jnp.where(named & inside, 1.0, 0.0)
        usable = jnp.where(row_step == t, flag, usable)
    mask[...] = usable
    loads[0].wait()
    loads[1].wait()

    def attend(d):
        keep = mask[...] > 0.0
        scores = lax.dot_general(
            qbuf[d], cache[...], (((1,), (1,)), ((), ())), preferred_element_type=jnp.float32
        ) * score_scale
        scores = jnp.where(keep, scores, very_low)
        peak = jnp.max(scores, axis=1, keepdims=True).astype(jnp.bfloat16).astype(jnp.float32)
        raw = jnp.where(keep, jnp.exp(scores - peak), 0.0)
        total = jnp.sum(raw, axis=1, keepdims=True)
        summed = jnp.dot(
            raw.astype(jnp.bfloat16), cache[:, :LATENT], preferred_element_type=jnp.float32
        )
        high = total.astype(jnp.bfloat16).astype(jnp.float32)
        lane = lax.broadcasted_iota(jnp.int32, (rows, STATS), 1)
        stats = jnp.where(lane == 0, peak, jnp.where(lane == 1, high, total - high))
        part[d, :, :LATENT] = summed.astype(jnp.bfloat16)
        part[d, :, LATENT:] = stats.astype(jnp.bfloat16)

    def answer(d):
        query_copy(d).wait_recv()
        attend(d)
        part_copy(d).start()

    if n_seq <= 8:
        for d in order:
            answer(d)
        attend(0)
    else:
        pl.loop(1, n_seq)(answer)
        attend(0)

    def parts_of(ref, d):
        stats = ref[d, :, LATENT:].astype(jnp.float32)
        return (
            stats[:, 0:1], stats[:, 1:2] + stats[:, 2:3], ref[d, :, :LATENT].astype(jnp.float32)
        )

    def join(left, right):
        peak = jnp.maximum(left[0], right[0])
        scale_left = jnp.exp(left[0] - peak)
        scale_right = jnp.exp(right[0] - peak)
        return (
            peak,
            left[1] * scale_left + right[1] * scale_right,
            left[2] * scale_left + right[2] * scale_right,
        )

    def take(d, running):
        part_copy(d).wait_recv()
        return join(running, parts_of(got, d))

    running = parts_of(part, 0)
    if n_seq <= 8:
        for d in order:
            running = take(d, running)
    else:
        running = lax.fori_loop(1, n_seq, take, running)
    latent_out = (running[2] / running[1]).astype(jnp.bfloat16).astype(jnp.float32)
    for c in range(LATENT // LANES):
        lat[c] = latent_out[:, c * LANES:(c + 1) * LANES]

    loads[2].wait()
    for h in range(heads):
        pick = pl.ds(h, steps, stride=heads)
        row = jnp.concatenate([lat[c, pick, :] for c in range(LATENT // LANES)], axis=1)
        hf[pick, :] = jnp.dot(
            row.astype(jnp.bfloat16), wv[h], preferred_element_type=jnp.float32
        )
    hsend[...] = hf[...].astype(jnp.bfloat16)
    for e in range(1, n_req):
        head_copy(e).start()
    hall[req] = hsend[...]
    for e in range(1, n_req):
        head_copy(e).wait_recv()
    for r in range(n_req):
        hwide[r * rows:(r + 1) * rows, :] = hall[r].astype(jnp.float32)
    flat = jnp.concatenate(
        [hwide[pl.ds(h, n_req * steps, stride=heads), :] for h in range(heads)], axis=1
    ).astype(jnp.bfloat16)

    loads[3].wait()
    mixed = jnp.dot(flat, wo[...], preferred_element_type=jnp.float32)
    for j in range(n_seq):
        ysend[j] = mixed[:, j * cols:(j + 1) * cols]
    for d in order:
        out_copy(d).start()
    total = ysend[me]
    for d in order:
        out_copy(d).wait_recv()
        total = total + yrecv[d]
    out_ref[...] = total.T.astype(out_ref.dtype)

    for d in order:
        query_copy(d).wait_send()
        part_copy(d).wait_send()
        out_copy(d).wait_send()
    for e in range(1, n_req):
        head_copy(e).wait_send()


def body(n_seq, n_req, latent_cache, queries, chosen, position, w_value, w_out):
    req_dev, cache_len, width = latent_cache.shape
    assert req_dev == 1
    steps, heads = queries.shape[1], queries.shape[2]
    rows = steps * heads
    vdim = w_value.shape[2]
    cols = w_out.shape[1] // n_seq
    bf16, f32 = jnp.bfloat16, jnp.float32
    everywhere = pl.BlockSpec(memory_space=pl.ANY)
    scalars = pl.BlockSpec(memory_space=pltpu.SMEM)
    dma = pltpu.SemaphoreType.DMA
    return pl.pallas_call(
        functools.partial(kernel, n_seq, n_req, steps, heads),
        out_shape=jax.ShapeDtypeStruct((cols, n_req * steps), bf16),
        in_specs=[scalars, scalars] + [everywhere] * 4,
        out_specs=pl.BlockSpec(memory_space=pltpu.VMEM),
        scratch_shapes=[
            pltpu.VMEM((n_seq, rows, width), bf16),
            pltpu.VMEM((cache_len, width), bf16),
            pltpu.VMEM(w_value.shape, bf16),
            pltpu.VMEM(w_out.shape, bf16),
            pltpu.VMEM((rows, cache_len), f32),
            pltpu.VMEM((n_seq, rows, LATENT + STATS), bf16),
            pltpu.VMEM((n_seq, rows, LATENT + STATS), bf16),
            pltpu.VMEM((LATENT // LANES, rows, LANES), f32),
            pltpu.VMEM((rows, vdim), f32),
            pltpu.VMEM((rows, vdim), bf16),
            pltpu.VMEM((n_req, rows, vdim), bf16),
            pltpu.VMEM((n_req * rows, vdim), f32),
            pltpu.VMEM((n_seq, n_req * steps, cols), f32),
            pltpu.VMEM((n_seq, n_req * steps, cols), f32),
            dma((4,)),
            dma((n_seq,)), dma((n_seq,)), dma((n_seq,)), dma((n_seq,)),
            dma((n_req,)), dma((n_req,)), dma((n_seq,)), dma((n_seq,)),
        ],
        compiler_params=pltpu.CompilerParams(
            collective_id=0, has_side_effects=True, vmem_limit_bytes=60 << 20
        ),
    )(
        chosen.reshape(steps, chosen.shape[2]),
        position,
        queries.reshape(rows, width),
        latent_cache.reshape(cache_len, width),
        w_value,
        w_out,
    )


def solution(mesh):
    return jax.shard_map(
        functools.partial(body, mesh.shape["seq"], mesh.shape["req"]),
        mesh=mesh,
        in_specs=(
            P("req", "seq", None),
            P("req", None, "seq", None),
            P("req", None, None),
            P("req"),
            P("seq", None, None),
            P("seq", "req"),
        ),
        out_specs=P(("req", "seq"), None),
        check_vma=False,
    )
```

time: 253 us -> 46.3 us (0.18)
  waiting for transfers between devices: 108 us -> 0 us
  blocking collectives: 92.3 us -> 0 us
  Pallas kernels: 0 us -> 40.5 us
  other arithmetic: 14.2 us -> 0 us
  between operations: 14.1 us -> 0.66 us
  local copies, waits for them, and re-layouts: 16.4 us -> 4.91 us
  matrix products: 6.84 us -> 0 us
    all_gather x4 -> x0, blocking collectives: 92.3 us -> none  [the longest x2 53.9 us: joined(): pieces = jax.tree.map(lambda part: lax.all_gather(part, axis), value)]
    unnamed x3 -> x0, waiting for transfers between devices: 62.4 us -> none
    all_gather x1 -> x0, waiting for transfers between devices: 46 us -> none  [joined(): pieces = jax.tree.map(lambda part: lax.all_gather(part, axis), value)]
    pallas_call x0 -> x1, Pallas kernels: none -> 40.5 us  [body(): pl.pallas_call(functools.partial(kernel, n_seq, n_req, steps, heads), out...]
    add x14 -> x0, other arithmetic: 9.73 us -> none  [the longest x7 9.56 us: join_parts(): summed_left * factor_left[:, :, None]]
    dot_general x4 -> x0, matrix products: 6.84 us -> none  [the longest x1 4.14 us: body(): lax.dot_general(w_out, flat_heads, (((0,), (1,)), ((), ())), preferred_el...]
    slice x7 -> x0, local copies, waits for them, and re-layouts: 6.06 us -> none  [the longest x3 6.05 us: joined(): tail = jax.tree.map(lambda part: part[1:], pieces)]
    gather x1 -> x0, local copies, waits for them, and re-layouts: 5.55 us -> none  [body(): jnp.take(latent_cache.reshape(req_dev * cache_len, key_width), flat_rows,...]
  transfers between devices with their start and end apart: 2 -> 0, of which waited for: 2 -> 0; matrix products, arithmetic and copies ran while one was open for 0% -> 0% of each run, Pallas kernels for 0% -> 0%
where the time goes in v1:
time: 46.3 us; the launch traced here: 46 us
  Pallas kernels  40.5 us (87%)
  local copies, waits for them, and re-layouts  4.91 us (11%)
  between operations  0.66 us (1%)
    pallas_call x1, Pallas kernels, body(): pl.pallas_call(functools.partial(kernel, n_seq, n_req, steps, heads), out...  40.5 us
    unnamed x2, local copies, waits for them, and re-layouts  3.4 us
    pallas_call x1, local copies, waits for them, and re-layouts, body(): pl.pallas_call(functools.partial(kernel, n_seq, n_req, steps, heads), out...  1.51 us

profile of v1, /device:TPU:0, one launch (start us, length us, event | category | flops | bytes accessed | tf_op | source)
XLA Modules:
  0.0 46.0 jit_solution(13009157688717664196)
XLA Ops:
  0.7 1.3 %copy.11 = s32[1,3,32]{2,1,0:T(4,128)} copy(s32[1,3,32]{2,0,1:T(1,128)} %param.8) | data formatting | bytes 768
  1.9 2.1 %copy.7 = bf16[1,512,576]{2,1,0:T(8,128)(2,1)} copy(bf16[1,512,576]{1,2,0:T(8,128)(2,1)} %param.6) | data formatting | bytes 1179648 | tf_op args[0]
  4.1 40.5 %shard_map.64 = bf16[224,12]{1,0:T(8,128)(2,1)} custom-call(s32[3,32]{1,0:T(4,128)} %bitcast.7, s32[1]{0:T(128)S(6)} %copy.12.position_ref, bf16[48,576]{1,0:T(8,128)(2,1)} %bitcast.6, bf16[512,576]{1,0:T(8,128)(2,1)} %bitcast.5, bf16[16,512,128]{2,1,0:T(8,128)(2,1)} %wv_hbm.1, bf16[2048,1792]{1,0:T(8,128)(2,1)} %wo_hbm.1), custom_call_target="tpu_custom_call" | custom-call | tf_op jit(solution)/shard_map/pallas_call | solution.py:212
  44.5 1.5 %copy.8 = bf16[224,12]{0,1:T(8,128)(2,1)} copy(bf16[224,12]{1,0:T(8,128)(2,1)} %shard_map.64) | data formatting | bytes 10752 | tf_op jit(solution)/shard_map/pallas_call | solution.py:212

commit v2 on v1

--- a/solution.py
+++ b/solution.py
@@ -28,7 +28,7 @@
     me = lax.axis_index("seq")
     req = lax.axis_index("req")
     rows = steps * heads
-    cache_len = cache.shape[0]
+    cache_len = cache.shape[1]
     cols = ysend.shape[2]
 
     loads = [
@@ -89,9 +89,9 @@
     row_step = lax.broadcasted_iota(jnp.int32, (rows, cache_len), 0) // heads
     usable = jnp.zeros((rows, cache_len), jnp.float32)
     for t in range(steps):
-        named = block == chosen_ref[t, 0]
-        for k in range(1, chosen_ref.shape[1]):
-            named = named | (block == chosen_ref[t, k])
+        named = block == chosen_ref[t, 0, 0]
+        for k in range(1, chosen_ref.shape[2]):
+            named = named | (block == chosen_ref[t, 0, k])
         flag = jnp.where(named & inside, 1.0, 0.0)
         usable = jnp.where(row_step == t, flag, usable)
     mask[...] = usable
@@ -101,14 +101,15 @@
     def attend(d):
         keep = mask[...] > 0.0
         scores = lax.dot_general(
-            qbuf[d], cache[...], (((1,), (1,)), ((), ())), preferred_element_type=jnp.float32
+            qbuf[d], cache[...], (((1,), (0,)), ((), ())), preferred_element_type=jnp.float32
         ) * score_scale
         scores = jnp.where(keep, scores, very_low)
         peak = jnp.max(scores, axis=1, keepdims=True).astype(jnp.bfloat16).astype(jnp.float32)
         raw = jnp.where(keep, jnp.exp(scores - peak), 0.0)
         total = jnp.sum(raw, axis=1, keepdims=True)
-        summed = jnp.dot(
-            raw.astype(jnp.bfloat16), cache[:, :LATENT], preferred_element_type=jnp.float32
+        summed = lax.dot_general(
+            raw.astype(jnp.bfloat16), cache[:LATENT, :], (((1,), (1,)), ((), ())),
+            preferred_element_type=jnp.float32,
         )
         high = total.astype(jnp.bfloat16).astype(jnp.float32)
         lane = lax.broadcasted_iota(jnp.int32, (rows, STATS), 1)
@@ -188,7 +189,7 @@
     for d in order:
         out_copy(d).wait_recv()
         total = total + yrecv[d]
-    out_ref[...] = total.T.astype(out_ref.dtype)
+    out_ref[...] = total
 
     for d in order:
         query_copy(d).wait_send()
@@ -209,14 +210,14 @@
     everywhere = pl.BlockSpec(memory_space=pl.ANY)
     scalars = pl.BlockSpec(memory_space=pltpu.SMEM)
     dma = pltpu.SemaphoreType.DMA
-    return pl.pallas_call(
+    mixed_out = pl.pallas_call(
         functools.partial(kernel, n_seq, n_req, steps, heads),
-        out_shape=jax.ShapeDtypeStruct((cols, n_req * steps), bf16),
+        out_shape=jax.ShapeDtypeStruct((n_req * steps, cols), f32),
         in_specs=[scalars, scalars] + [everywhere] * 4,
         out_specs=pl.BlockSpec(memory_space=pltpu.VMEM),
         scratch_shapes=[
             pltpu.VMEM((n_seq, rows, width), bf16),
-            pltpu.VMEM((cache_len, width), bf16),
+            pltpu.VMEM((width, cache_len), bf16),
             pltpu.VMEM(w_value.shape, bf16),
             pltpu.VMEM(w_out.shape, bf16),
             pltpu.VMEM((rows, cache_len), f32),
@@ -237,13 +238,14 @@
             collective_id=0, has_side_effects=True, vmem_limit_bytes=60 << 20
         ),
     )(
-        chosen.reshape(steps, chosen.shape[2]),
+        chosen.transpose(1, 0, 2),
         position,
         queries.reshape(rows, width),
-        latent_cache.reshape(cache_len, width),
+        latent_cache.reshape(cache_len, width).T,
         w_value,
         w_out,
     )
+    return mixed_out.T.astype(bf16)
 
 
 def solution(mesh):

time: 46.3 us -> 42.6 us (0.920)
  local copies, waits for them, and re-layouts: 4.91 us -> 0 us
  other arithmetic: 0 us -> 1.32 us
    unnamed x2 -> x0, local copies, waits for them, and re-layouts: 3.4 us -> none
    pallas_call x1 -> x0, local copies, waits for them, and re-layouts: 1.51 us -> none  [body(): pl.pallas_call(functools.partial(kernel, n_seq, n_req, steps, heads), out...]
    convert_element_type x0 -> x1, other arithmetic: none -> 1.32 us  [body(): return mixed_out.T.astype(bf16)]
where the time goes in v2:
time: 42.6 us; the launch traced here: 42.3 us
  Pallas kernels  40.4 us (95%)
  other arithmetic  1.32 us (3%)
  between operations  0.66 us (2%)
    pallas_call x1, Pallas kernels, body(): pl.pallas_call(functools.partial(kernel, n_seq, n_req, steps, heads), out...  40.4 us
    convert_element_type x1, other arithmetic, body(): return mixed_out.T.astype(bf16)  1.32 us

profile of v2, /device:TPU:0, one launch (start us, length us, event | category | flops | bytes accessed | tf_op | source)
XLA Modules:
  0.0 42.3 jit_solution(7772258215628999747)
XLA Ops:
  0.7 40.4 %shard_map.64 = f32[12,224]{1,0:T(8,128)} custom-call(s32[3,1,32]{2,1,0:T(1,128)} %bitcast.9, s32[1]{0:T(128)S(6)} %copy.7.position_ref, bf16[48,576]{1,0:T(8,128)(2,1)} %bitcast.8, bf16[576,512]{1,0:T(8,128)(2,1)} %bitcast.7, bf16[16,512,128]{2,1,0:T(8,128)(2,1)} %wv_hbm.1, bf16[2048,1792]{1,0:T(8,128)(2,1)} %wo_hbm.1), custom_call_target="tpu_custom_call" | custom-call | tf_op jit(solution)/shard_map/pallas_call | solution.py:213
  41.0 1.3 %convert_bitcast_fusion = bf16[224,12]{0,1:T(8,128)(2,1)} fusion(f32[12,224]{1,0:T(8,128)} %shard_map.64), kind=kLoop, calls=%fused_computation | loop fusion | flops 2688 | bytes 16128 | tf_op jit(solution)/shard_map/convert_element_type | solution.py:248

commit v3 on v2

v3 whole, which is shorter than its diff:
```python
import functools
import math

import jax
import jax.numpy as jnp
from jax import lax
from jax.experimental import pallas as pl
from jax.experimental.pallas import tpu as pltpu
from jax.sharding import PartitionSpec as P

LATENT = 512
BLOCK = 64
LANES = 128
STATS = 128
MESH = pl.DeviceIdType.MESH

score_scale = 1.0 / math.sqrt(192.0)
very_low = -1e30


def kernel(
    n_seq, n_req, steps, heads,
    chosen_ref, position_ref, q_hbm, cache_hbm, wv_hbm, wo_hbm,
    out_ref,
    qbuf, cache, wv, wo, mask, part, pair, joint, got, lat, hf, hsend, hall, hwide, ysend, yrecv,
    load_sem, q_send, q_recv, f_send, f_recv, p_send, p_recv, j_send, j_recv,
    h_send, h_recv, y_send, y_recv,
):
    me = lax.axis_index("seq")
    req = lax.axis_index("req")
    rows = steps * heads
    cache_len = cache.shape[1]
    cols = ysend.shape[2]
    groups = n_seq // 2
    group, side = me // 2, me % 2

    loads = [
        pltpu.make_async_copy(q_hbm, qbuf.at[0, 0], load_sem.at[0]),
        pltpu.make_async_copy(cache_hbm, cache, load_sem.at[1]),
        pltpu.make_async_copy(wv_hbm, wv, load_sem.at[2]),
        pltpu.make_async_copy(wo_hbm, wo, load_sem.at[3]),
    ]
    loads[0].start()
    loads[1].start()

    def seq_at(offset):
        return {"seq": lax.rem(me + offset, n_seq)}

    def req_at(offset):
        return {"req": lax.rem(req + offset, n_req)}

    def column(k):
        other, bit = 0, 1
        while bit < groups:
            own = (group // bit) % 2
            other = other + bit * ((1 - own) if k & bit else own)
            bit *= 2
        return {"seq": 2 * other + side}

    partner = {"seq": 2 * group + 1 - side}

    barrier = pltpu.get_barrier_semaphore()
    for d in range(1, n_seq):
        pl.semaphore_signal(barrier, inc=1, device_id=seq_at(d), device_id_type=MESH)
    for e in range(1, n_req):
        pl.semaphore_signal(barrier, inc=1, device_id=req_at(e), device_id_type=MESH)

    block = me * (cache_len // BLOCK) + lax.broadcasted_iota(jnp.int32, (1, cache_len), 1) // BLOCK
    inside = me * cache_len + lax.broadcasted_iota(jnp.int32, (1, cache_len), 1) < position_ref[0]
    row_step = lax.broadcasted_iota(jnp.int32, (rows, cache_len), 0) // heads
    usable = jnp.zeros((rows, cache_len), jnp.float32)
    for t in range(steps):
        named = block == chosen_ref[t, 0, 0]
        for k in range(1, chosen_ref.shape[2]):
            named = named | (block == chosen_ref[t, 0, k])
        flag = jnp.where(named & inside, 1.0, 0.0)
        usable = jnp.where(row_step == t, flag, usable)
    mask[...] = usable
    pl.semaphore_wait(barrier, n_seq + n_req - 2)

    def remote(src, dst, send, recv, device):
        return pltpu.make_async_remote_copy(
            src_ref=src, dst_ref=dst, send_sem=send, recv_sem=recv,
            device_id=device, device_id_type=MESH,
        )

    def query_copy(k):
        return remote(q_hbm, qbuf.at[k, 0], q_send.at[k], q_recv.at[k], column(k))

    def forward_copy(k):
        src = qbuf.at[k, 0] if k else q_hbm
        return remote(src, qbuf.at[k, 1], f_send.at[k], f_recv.at[k], partner)

    def pair_copy(k):
        return remote(part.at[k, 1], pair.at[k], p_send.at[k], p_recv.at[k], partner)

    def joint_copy(k):
        return remote(joint.at[k], got.at[k], j_send.at[k], j_recv.at[k], column(k))

    def head_copy(e):
        return remote(hsend, hall.at[req], h_send.at[e], h_recv.at[e], req_at(e))

    def out_copy(d):
        return remote(
            ysend.at[lax.rem(me + d, n_seq)], yrecv.at[d], y_send.at[d], y_recv.at[d], seq_at(d)
        )

    order = sorted(range(1, n_seq), key=lambda d: (min(d, n_seq - d), d))
    forward_copy(0).start()
    for k in range(1, groups):
        query_copy(k).start()
    loads[2].start()
    loads[3].start()
    loads[0].wait()
    loads[1].wait()

    def store(ref, at, peak, total, summed):
        high = total.astype(jnp.bfloat16).astype(jnp.float32)
        lane = lax.broadcasted_iota(jnp.int32, (rows, STATS), 1)
        stats = jnp.where(lane == 0, peak, jnp.where(lane == 1, high, total - high))
        ref[at + (slice(None), slice(0, LATENT))] = summed.astype(jnp.bfloat16)
        ref[at + (slice(None), slice(LATENT, LATENT + STATS))] = stats.astype(jnp.bfloat16)

    def load(ref, at):
        stats = ref[at + (slice(None), slice(LATENT, LATENT + STATS))].astype(jnp.float32)
        return (
            stats[:, 0:1],
            stats[:, 1:2] + stats[:, 2:3],
            ref[at + (slice(None), slice(0, LATENT))].astype(jnp.float32),
        )

    def attend(k, j):
        keep = mask[...] > 0.0
        scores = lax.dot_general(
            qbuf[k, j], cache[...], (((1,), (0,)), ((), ())), preferred_element_type=jnp.float32
        ) * score_scale
        scores = jnp.where(keep, scores, very_low)
        peak = jnp.max(scores, axis=1, keepdims=True).astype(jnp.bfloat16).astype(jnp.float32)
        raw = jnp.where(keep, jnp.exp(scores - peak), 0.0)
        total = jnp.sum(raw, axis=1, keepdims=True)
        summed = lax.dot_general(
            raw.astype(jnp.bfloat16), cache[:LATENT, :], (((1,), (1,)), ((), ())),
            preferred_element_type=jnp.float32,
        )
        store(part, (k, j), peak, total, summed)

    def join(left, right):
        peak = jnp.maximum(left[0], right[0])
        scale_left = jnp.exp(left[0] - peak)
        scale_right = jnp.exp(right[0] - peak)
        return (
            peak,
            left[1] * scale_left + right[1] * scale_right,
            left[2] * scale_left + right[2] * scale_right,
        )

    def serve_partner(k):
        forward_copy(k).wait_recv()
        attend(k, 1)
        pair_copy(k).start()

    def joined(k):
        pair_copy(k).wait_recv()
        return join(load(part, (k, 0)), load(pair, (k,)))

    def send_joint(k):
        store(joint, (k,), *joined(k))
        joint_copy(k).start()

    attend(0, 0)
    for k in range(1, groups):
        query_copy(k).wait_recv()
        forward_copy(k).start()
        if k >= 2:
            serve_partner(k - 1)
        attend(k, 0)
        if k >= 3:
            send_joint(k - 2)
    serve_partner(groups - 1)
    serve_partner(0)
    for k in range(max(1, groups - 2), groups):
        send_joint(k)
    running = joined(0)
    for k in range(1, groups):
        joint_copy(k).wait_recv()
        running = join(running, load(got, (k,)))
    latent_out = (running[2] / running[1]).astype(jnp.bfloat16).astype(jnp.float32)
    for c in range(LATENT // LANES):
        lat[c] = latent_out[:, c * LANES:(c + 1) * LANES]

    loads[2].wait()
    for h in range(heads):
        pick = pl.ds(h, steps, stride=heads)
        row = jnp.concatenate([lat[c, pick, :] for c in range(LATENT // LANES)], axis=1)
        hf[pick, :] = jnp.dot(
            row.astype(jnp.bfloat16), wv[h], preferred_element_type=jnp.float32
        )
    hsend[...] = hf[...].astype(jnp.bfloat16)
    for e in range(1, n_req):
        head_copy(e).start()
    hall[req] = hsend[...]
    for e in range(1, n_req):
        head_copy(e).wait_recv()
    for r in range(n_req):
        hwide[r * rows:(r + 1) * rows, :] = hall[r].astype(jnp.float32)
    flat = jnp.concatenate(
        [hwide[pl.ds(h, n_req * steps, stride=heads), :] for h in range(heads)], axis=1
    ).astype(jnp.bfloat16)

    loads[3].wait()
    mixed = jnp.dot(flat, wo[...], preferred_element_type=jnp.float32)
    for j in range(n_seq):
        ysend[j] = mixed[:, j * cols:(j + 1) * cols].astype(jnp.bfloat16)
    for d in order:
        out_copy(d).start()
    total = ysend[me].astype(jnp.float32)
    for d in order:
        out_copy(d).wait_recv()
        total = total + yrecv[d].astype(jnp.float32)
    out_ref[...] = total

    for k in range(groups):
        forward_copy(k).wait_send()
        pair_copy(k).wait_send()
    for k in range(1, groups):
        query_copy(k).wait_send()
        joint_copy(k).wait_send()
    for d in order:
        out_copy(d).wait_send()
    for e in range(1, n_req):
        head_copy(e).wait_send()


def body(n_seq, n_req, latent_cache, queries, chosen, position, w_value, w_out):
    req_dev, cache_len, width = latent_cache.shape
    assert req_dev == 1
    steps, heads = queries.shape[1], queries.shape[2]
    rows = steps * heads
    groups = n_seq // 2
    assert n_seq == 2 * groups and groups & (groups - 1) == 0
    vdim = w_value.shape[2]
    cols = w_out.shape[1] // n_seq
    bf16, f32 = jnp.bfloat16, jnp.float32
    everywhere = pl.BlockSpec(memory_space=pl.ANY)
    scalars = pl.BlockSpec(memory_space=pltpu.SMEM)
    dma = pltpu.SemaphoreType.DMA
    mixed_out = pl.pallas_call(
        functools.partial(kernel, n_seq, n_req, steps, heads),
        out_shape=jax.ShapeDtypeStruct((n_req * steps, cols), f32),
        in_specs=[scalars, scalars] + [everywhere] * 4,
        out_specs=pl.BlockSpec(memory_space=pltpu.VMEM),
        scratch_shapes=[
            pltpu.VMEM((groups, 2, rows, width), bf16),
            pltpu.VMEM((width, cache_len), bf16),
            pltpu.VMEM(w_value.shape, bf16),
            pltpu.VMEM(w_out.shape, bf16),
            pltpu.VMEM((rows, cache_len), f32),
            pltpu.VMEM((groups, 2, rows, LATENT + STATS), bf16),
            pltpu.VMEM((groups, rows, LATENT + STATS), bf16),
            pltpu.VMEM((groups, rows, LATENT + STATS), bf16),
            pltpu.VMEM((groups, rows, LATENT + STATS), bf16),
            pltpu.VMEM((LATENT // LANES, rows, LANES), f32),
            pltpu.VMEM((rows, vdim), f32),
            pltpu.VMEM((rows, vdim), bf16),
            pltpu.VMEM((n_req, rows, vdim), bf16),
            pltpu.VMEM((n_req * rows, vdim), f32),
            pltpu.VMEM((n_seq, n_req * steps, cols), bf16),
            pltpu.VMEM((n_seq, n_req * steps, cols), bf16),
            dma((4,)),
            dma((groups,)), dma((groups,)), dma((groups,)), dma((groups,)),
            dma((groups,)), dma((groups,)), dma((groups,)), dma((groups,)),
            dma((n_req,)), dma((n_req,)), dma((n_seq,)), dma((n_seq,)),
        ],
        compiler_params=pltpu.CompilerParams(
            collective_id=0, has_side_effects=True, vmem_limit_bytes=60 << 20
        ),
    )(
        chosen.transpose(1, 0, 2),
        position,
        queries.reshape(rows, width),
        latent_cache.reshape(cache_len, width).T,
        w_value,
        w_out,
    )
    return mixed_out.T.astype(bf16)


def solution(mesh):
    return jax.shard_map(
        functools.partial(body, mesh.shape["seq"], mesh.shape["req"]),
        mesh=mesh,
        in_specs=(
            P("req", "seq", None),
            P("req", None, "seq", None),
            P("req", None, None),
            P("req"),
            P("seq", None, None),
            P("seq", "req"),
        ),
        out_specs=P(("req", "seq"), None),
        check_vma=False,
    )
```

time: 42.6 us -> 39.4 us (0.925)
  Pallas kernels: 40.4 us -> 37.1 us
    pallas_call x1, Pallas kernels: 40.4 us -> 37.1 us  [body(): pl.pallas_call(functools.partial(kernel, n_seq, n_req, steps, heads), out...]
where the time goes in v3:
time: 39.4 us; the launch traced here: 39.1 us
  Pallas kernels  37.1 us (94%)
  other arithmetic  1.32 us (3%)
  between operations  0.66 us (2%)
    pallas_call x1, Pallas kernels, body(): pl.pallas_call(functools.partial(kernel, n_seq, n_req, steps, heads), out...  37.1 us
    convert_element_type x1, other arithmetic, body(): return mixed_out.T.astype(bf16)  1.32 us

profile of v3, /device:TPU:0, one launch (start us, length us, event | category | flops | bytes accessed | tf_op | source)
XLA Modules:
  0.0 39.1 jit_solution(670547098789664875)
XLA Ops:
  0.7 37.1 %shard_map.64 = f32[12,224]{1,0:T(8,128)} custom-call(s32[3,1,32]{2,1,0:T(1,128)} %bitcast.9, s32[1]{0:T(128)S(6)} %copy.7.position_ref, bf16[48,576]{1,0:T(8,128)(2,1)} %bitcast.8, bf16[576,512]{1,0:T(8,128)(2,1)} %bitcast.7, bf16[16,512,128]{2,1,0:T(8,128)(2,1)} %wv_hbm.1, bf16[2048,1792]{1,0:T(8,128)(2,1)} %wo_hbm.1), custom_call_target="tpu_custom_call" | custom-call | tf_op jit(solution)/shard_map/pallas_call | solution.py:247
  37.8 1.3 %convert_bitcast_fusion = bf16[224,12]{0,1:T(8,128)(2,1)} fusion(f32[12,224]{1,0:T(8,128)} %shard_map.64), kind=kLoop, calls=%fused_computation | loop fusion | flops 2688 | bytes 16128 | tf_op jit(solution)/shard_map/convert_element_type | solution.py:285

commit v4 on v3

--- a/solution.py
+++ b/solution.py
@@ -11,6 +11,7 @@
 LATENT = 512
 BLOCK = 64
 LANES = 128
+HALVES = 2
 STATS = 128
 MESH = pl.DeviceIdType.MESH
 
@@ -22,20 +23,21 @@
     n_seq, n_req, steps, heads,
     chosen_ref, position_ref, q_hbm, cache_hbm, wv_hbm, wo_hbm,
     out_ref,
-    qbuf, cache, wv, wo, mask, part, pair, joint, got, lat, hf, hsend, hall, hwide, ysend, yrecv,
+    own, qbuf, cache, wv, wo, mask, part, pair, joint, got, lat, hf, hsend, hall, hwide, ysend, yrecv,
     load_sem, q_send, q_recv, f_send, f_recv, p_send, p_recv, j_send, j_recv,
     h_send, h_recv, y_send, y_recv,
 ):
     me = lax.axis_index("seq")
     req = lax.axis_index("req")
     rows = steps * heads
+    part_rows = rows // HALVES
     cache_len = cache.shape[1]
-    cols = ysend.shape[2]
+    outs, cols = out_ref.shape
     groups = n_seq // 2
     group, side = me // 2, me % 2
 
     loads = [
-        pltpu.make_async_copy(q_hbm, qbuf.at[0, 0], load_sem.at[0]),
+        pltpu.make_async_copy(q_hbm, own, load_sem.at[0]),
         pltpu.make_async_copy(cache_hbm, cache, load_sem.at[1]),
         pltpu.make_async_copy(wv_hbm, wv, load_sem.at[2]),
         pltpu.make_async_copy(wo_hbm, wo, load_sem.at[3]),
@@ -75,7 +77,8 @@
             named = named | (block == chosen_ref[t, 0, k])
         flag = jnp.where(named & inside, 1.0, 0.0)
         usable = jnp.where(row_step == t, flag, usable)
-    mask[...] = usable
+    for p in range(HALVES):
+        mask[p] = usable[p * part_rows:(p + 1) * part_rows]
     pl.semaphore_wait(barrier, n_seq + n_req - 2)
 
     def remote(src, dst, send, recv, device):
@@ -84,18 +87,25 @@
             device_id=device, device_id_type=MESH,
         )
 
-    def query_copy(k):
-        return remote(q_hbm, qbuf.at[k, 0], q_send.at[k], q_recv.at[k], column(k))
-
-    def forward_copy(k):
-        src = qbuf.at[k, 0] if k else q_hbm
-        return remote(src, qbuf.at[k, 1], f_send.at[k], f_recv.at[k], partner)
-
-    def pair_copy(k):
-        return remote(part.at[k, 1], pair.at[k], p_send.at[k], p_recv.at[k], partner)
-
-    def joint_copy(k):
-        return remote(joint.at[k], got.at[k], j_send.at[k], j_recv.at[k], column(k))
+    def slot(p, k):
+        return p * groups + k
+
+    def query_copy(p, k):
+        i = slot(p, k)
+        return remote(q_hbm.at[p], qbuf.at[i, 0], q_send.at[i], q_recv.at[i], column(k))
+
+    def forward_copy(p, k):
+        i = slot(p, k)
+        src = qbuf.at[i, 0] if k else q_hbm.at[p]
+        return remote(src, qbuf.at[i, 1], f_send.at[i], f_recv.at[i], partner)
+
+    def pair_copy(p, k):
+        i = slot(p, k)
+        return remote(part.at[i, 1], pair.at[i], p_send.at[i], p_recv.at[i], partner)
+
+    def joint_copy(p, k):
+        i = slot(p, k)
+        return remote(joint.at[i], got.at[i], j_send.at[i], j_recv.at[i], column(k))
 
     def head_copy(e):
         return remote(hsend, hall.at[req], h_send.at[e], h_recv.at[e], req_at(e))
@@ -105,10 +115,11 @@
             ysend.at[lax.rem(me + d, n_seq)], yrecv.at[d], y_send.at[d], y_recv.at[d], seq_at(d)
         )
 
-    order = sorted(range(1, n_seq), key=lambda d: (min(d, n_seq - d), d))
-    forward_copy(0).start()
-    for k in range(1, groups):
-        query_copy(k).start()
+    order = sorted(range(1, n_seq), key=lambda d: (-min(d, n_seq - d), d))
+    for p in range(HALVES):
+        forward_copy(p, 0).start()
+        for k in range(1, groups):
+            query_copy(p, k).start()
     loads[2].start()
     loads[3].start()
     loads[0].wait()
@@ -116,7 +127,7 @@
 
     def store(ref, at, peak, total, summed):
         high = total.astype(jnp.bfloat16).astype(jnp.float32)
-        lane = lax.broadcasted_iota(jnp.int32, (rows, STATS), 1)
+        lane = lax.broadcasted_iota(jnp.int32, (part_rows, STATS), 1)
         stats = jnp.where(lane == 0, peak, jnp.where(lane == 1, high, total - high))
         ref[at + (slice(None), slice(0, LATENT))] = summed.astype(jnp.bfloat16)
         ref[at + (slice(None), slice(LATENT, LATENT + STATS))] = stats.astype(jnp.bfloat16)
@@ -129,10 +140,12 @@
             ref[at + (slice(None), slice(0, LATENT))].astype(jnp.float32),
         )
 
-    def attend(k, j):
-        keep = mask[...] > 0.0
+    def attend(p, k, j):
+        i = slot(p, k)
+        queries = own[p] if (k, j) == (0, 0) else qbuf[i, j]
+        keep = mask[p] > 0.0
         scores = lax.dot_general(
-            qbuf[k, j], cache[...], (((1,), (0,)), ((), ())), preferred_element_type=jnp.float32
+            queries, cache[...], (((1,), (0,)), ((), ())), preferred_element_type=jnp.float32
         ) * score_scale
         scores = jnp.where(keep, scores, very_low)
         peak = jnp.max(scores, axis=1, keepdims=True).astype(jnp.bfloat16).astype(jnp.float32)
@@ -142,7 +155,7 @@
             raw.astype(jnp.bfloat16), cache[:LATENT, :], (((1,), (1,)), ((), ())),
             preferred_element_type=jnp.float32,
         )
-        store(part, (k, j), peak, total, summed)
+        store(part, (i, j), peak, total, summed)
 
     def join(left, right):
         peak = jnp.maximum(left[0], right[0])
@@ -154,39 +167,50 @@
             left[2] * scale_left + right[2] * scale_right,
         )
 
-    def serve_partner(k):
-        forward_copy(k).wait_recv()
-        attend(k, 1)
-        pair_copy(k).start()
-
-    def joined(k):
-        pair_copy(k).wait_recv()
-        return join(load(part, (k, 0)), load(pair, (k,)))
-
-    def send_joint(k):
-        store(joint, (k,), *joined(k))
-        joint_copy(k).start()
-
-    attend(0, 0)
-    for k in range(1, groups):
-        query_copy(k).wait_recv()
-        forward_copy(k).start()
-        if k >= 2:
-            serve_partner(k - 1)
-        attend(k, 0)
-        if k >= 3:
-            send_joint(k - 2)
-    serve_partner(groups - 1)
-    serve_partner(0)
-    for k in range(max(1, groups - 2), groups):
-        send_joint(k)
-    running = joined(0)
-    for k in range(1, groups):
-        joint_copy(k).wait_recv()
-        running = join(running, load(got, (k,)))
-    latent_out = (running[2] / running[1]).astype(jnp.bfloat16).astype(jnp.float32)
-    for c in range(LATENT // LANES):
-        lat[c] = latent_out[:, c * LANES:(c + 1) * LANES]
+    def serve_column(p, k):
+        query_copy(p, k).wait_recv()
+        forward_copy(p, k).start()
+        attend(p, k, 0)
+
+    def serve_partner(p, k):
+        forward_copy(p, k).wait_recv()
+        attend(p, k, 1)
+        pair_copy(p, k).start()
+
+    def joined(p, k):
+        pair_copy(p, k).wait_recv()
+        return join(load(part, (slot(p, k), 0)), load(pair, (slot(p, k),)))
+
+    def send_joint(p, k):
+        store(joint, (slot(p, k),), *joined(p, k))
+        joint_copy(p, k).start()
+
+    others = range(1, groups)
+    for p in range(HALVES):
+        attend(p, 0, 0)
+    for p in range(HALVES):
+        serve_partner(p, 0)
+    for k in others:
+        serve_column(0, k)
+    for p in range(HALVES):
+        for k in others:
+            if p + 1 < HALVES:
+                serve_column(p + 1, k)
+            serve_partner(p, k)
+            if p:
+                send_joint(p - 1, k)
+    for k in others:
+        send_joint(HALVES - 1, k)
+    for p in range(HALVES):
+        running = joined(p, 0)
+        for k in others:
+            joint_copy(p, k).wait_recv()
+            running = join(running, load(got, (slot(p, k),)))
+        latent_out = (running[2] / running[1]).astype(jnp.bfloat16).astype(jnp.float32)
+        for c in range(LATENT // LANES):
+            lat[c, p * part_rows:(p + 1) * part_rows, :] = (
+                latent_out[:, c * LANES:(c + 1) * LANES]
+            )
 
     loads[2].wait()
     for h in range(heads):
@@ -210,21 +234,22 @@
     loads[3].wait()
     mixed = jnp.dot(flat, wo[...], preferred_element_type=jnp.float32)
     for j in range(n_seq):
-        ysend[j] = mixed[:, j * cols:(j + 1) * cols].astype(jnp.bfloat16)
+        ysend[j, :outs, :cols] = mixed[:, j * cols:(j + 1) * cols].astype(jnp.bfloat16)
     for d in order:
         out_copy(d).start()
     total = ysend[me].astype(jnp.float32)
     for d in order:
         out_copy(d).wait_recv()
         total = total + yrecv[d].astype(jnp.float32)
-    out_ref[...] = total
-
-    for k in range(groups):
-        forward_copy(k).wait_send()
-        pair_copy(k).wait_send()
-    for k in range(1, groups):
-        query_copy(k).wait_send()
-        joint_copy(k).wait_send()
+    out_ref[...] = total[:outs, :cols]
+
+    for p in range(HALVES):
+        for k in range(groups):
+            forward_copy(p, k).wait_send()
+            pair_copy(p, k).wait_send()
+        for k in others:
+            query_copy(p, k).wait_send()
+            joint_copy(p, k).wait_send()
     for d in order:
         out_copy(d).wait_send()
     for e in range(1, n_req):
@@ -237,9 +262,13 @@
     steps, heads = queries.shape[1], queries.shape[2]
     rows = steps * heads
     groups = n_seq // 2
+    slots, part_rows = HALVES * groups, rows // HALVES
+    assert rows == HALVES * part_rows
     assert n_seq == 2 * groups and groups & (groups - 1) == 0
     vdim = w_value.shape[2]
     cols = w_out.shape[1] // n_seq
+    out_rows = -(-n_req * steps // 16) * 16
+    out_lanes = -(-cols // LANES) * LANES
     bf16, f32 = jnp.bfloat16, jnp.float32
     everywhere = pl.BlockSpec(memory_space=pl.ANY)
     scalars = pl.BlockSpec(memory_space=pltpu.SMEM)
@@ -250,25 +279,26 @@
         in_specs=[scalars, scalars] + [everywhere] * 4,
         out_specs=pl.BlockSpec(memory_space=pltpu.VMEM),
         scratch_shapes=[
-            pltpu.VMEM((groups, 2, rows, width), bf16),
+            pltpu.VMEM((HALVES, part_rows, width), bf16),
+            pltpu.VMEM((slots, 2, part_rows, width), bf16),
             pltpu.VMEM((width, cache_len), bf16),
             pltpu.VMEM(w_value.shape, bf16),
             pltpu.VMEM(w_out.shape, bf16),
-            pltpu.VMEM((rows, cache_len), f32),
-            pltpu.VMEM((groups, 2, rows, LATENT + STATS), bf16),
-            pltpu.VMEM((groups, rows, LATENT + STATS), bf16),
-            pltpu.VMEM((groups, rows, LATENT + STATS), bf16),
-            pltpu.VMEM((groups, rows, LATENT + STATS), bf16),
+            pltpu.VMEM((HALVES, part_rows, cache_len), f32),
+            pltpu.VMEM((slots, 2, part_rows, LATENT + STATS), bf16),
+            pltpu.VMEM((slots, part_rows, LATENT + STATS), bf16),
+            pltpu.VMEM((slots, part_rows, LATENT + STATS), bf16),
+            pltpu.VMEM((slots, part_rows, LATENT + STATS), bf16),
             pltpu.VMEM((LATENT // LANES, rows, LANES), f32),
             pltpu.VMEM((rows, vdim), f32),
             pltpu.VMEM((rows, vdim), bf16),
             pltpu.VMEM((n_req, rows, vdim), bf16),
             pltpu.VMEM((n_req * rows, vdim), f32),
-            pltpu.VMEM((n_seq, n_req * steps, cols), bf16),
-            pltpu.VMEM((n_seq, n_req * steps, cols), bf16),
+            pltpu.VMEM((n_seq, out_rows, out_lanes), bf16),
+            pltpu.VMEM((n_seq, out_rows, out_lanes), bf16),
             dma((4,)),
-            dma((groups,)), dma((groups,)), dma((groups,)), dma((groups,)),
-            dma((groups,)), dma((groups,)), dma((groups,)), dma((groups,)),
+            dma((slots,)), dma((slots,)), dma((slots,)), dma((slots,)),
+            dma((slots,)), dma((slots,)), dma((slots,)), dma((slots,)),
             dma((n_req,)), dma((n_req,)), dma((n_seq,)), dma((n_seq,)),
         ],
         compiler_params=pltpu.CompilerParams(
@@ -277,7 +307,7 @@
     )(
         chosen.transpose(1, 0, 2),
         position,
-        queries.reshape(rows, width),
+        queries.reshape(HALVES, part_rows, width),
         latent_cache.reshape(cache_len, width).T,
         w_value,
         w_out,

time: 39.4 us -> 39.8 us (1.010)
  Pallas kernels: 37.1 us -> 37.6 us
    pallas_call x1, Pallas kernels: 37.1 us -> 37.6 us  [body(): pl.pallas_call(functools.partial(kernel, n_seq, n_req, steps, heads), out...]
where the time goes in v4:
time: 39.8 us; the launch traced here: 39.5 us
  Pallas kernels  37.6 us (94%)
  other arithmetic  1.32 us (3%)
  between operations  0.66 us (2%)
    pallas_call x1, Pallas kernels, body(): pl.pallas_call(functools.partial(kernel, n_seq, n_req, steps, heads), out...  37.6 us
    convert_element_type x1, other arithmetic, body(): return mixed_out.T.astype(bf16)  1.32 us

profile of v4, /device:TPU:0, one launch (start us, length us, event | category | flops | bytes accessed | tf_op | source)
XLA Modules:
  0.0 39.5 jit_solution(8266668122348516289)
XLA Ops:
  0.7 37.6 %shard_map.64 = f32[12,224]{1,0:T(8,128)} custom-call(s32[3,1,32]{2,1,0:T(1,128)} %bitcast.9, s32[1]{0:T(128)S(6)} %copy.7.position_ref, bf16[2,24,576]{2,1,0:T(8,128)(2,1)} %bitcast.8, bf16[576,512]{1,0:T(8,128)(2,1)} %bitcast.7, bf16[16,512,128]{2,1,0:T(8,128)(2,1)} %wv_hbm.1, bf16[2048,1792]{1,0:T(8,128)(2,1)} %wo_hbm.1), custom_call_target="tpu_custom_call" | custom-call | tf_op jit(solution)/shard_map/pallas_call | solution.py:276
  38.2 1.3 %convert_bitcast_fusion = bf16[224,12]{0,1:T(8,128)(2,1)} fusion(f32[12,224]{1,0:T(8,128)} %shard_map.64), kind=kLoop, calls=%fused_computation | loop fusion | flops 2688 | bytes 16128 | tf_op jit(solution)/shard_map/convert_element_type | solution.py:315

commit v5 on v4

--- a/solution.py
+++ b/solution.py
@@ -11,7 +11,7 @@
 LATENT = 512
 BLOCK = 64
 LANES = 128
-HALVES = 2
+HALVES = 1
 STATS = 128
 MESH = pl.DeviceIdType.MESH
 
@@ -199,7 +199,9 @@
             serve_partner(p, k)
             if p:
                 send_joint(p - 1, k)
-    for k in others:
+            elif HALVES == 1 and k > 1:
+                send_joint(0, k - 1)
+    for k in others if HALVES > 1 else others[-1:]:
         send_joint(HALVES - 1, k)
     for p in range(HALVES):
         running = joined(p, 0)

time: 39.8 us -> 40.6 us (1.020)
  Pallas kernels: 37.6 us -> 38.3 us
    pallas_call x1, Pallas kernels: 37.6 us -> 38.3 us  [body(): pl.pallas_call(functools.partial(kernel, n_seq, n_req, steps, heads), out...]
where the time goes in v5:
time: 40.6 us; the launch traced here: 40.3 us
  Pallas kernels  38.3 us (94%)
  other arithmetic  1.32 us (3%)
  between operations  0.66 us (2%)
    pallas_call x1, Pallas kernels, body(): pl.pallas_call(functools.partial(kernel, n_seq, n_req, steps, heads), out...  38.3 us
    convert_element_type x1, other arithmetic, body(): return mixed_out.T.astype(bf16)  1.32 us

profile of v5, /device:TPU:0, one launch (start us, length us, event | category | flops | bytes accessed | tf_op | source)
XLA Modules:
  0.0 40.3 jit_solution(16103488399273753532)
XLA Ops:
  0.7 38.3 %shard_map.64 = f32[12,224]{1,0:T(8,128)} custom-call(s32[3,1,32]{2,1,0:T(1,128)} %bitcast.9, s32[1]{0:T(128)S(6)} %copy.7.position_ref, bf16[1,48,576]{2,1,0:T(8,128)(2,1)} %bitcast.8, bf16[576,512]{1,0:T(8,128)(2,1)} %bitcast.7, bf16[16,512,128]{2,1,0:T(8,128)(2,1)} %wv_hbm.1, bf16[2048,1792]{1,0:T(8,128)(2,1)} %wo_hbm.1), custom_call_target="tpu_custom_call" | custom-call | tf_op jit(solution)/shard_map/pallas_call | solution.py:278
  39.0 1.3 %convert_bitcast_fusion = bf16[224,12]{0,1:T(8,128)(2,1)} fusion(f32[12,224]{1,0:T(8,128)} %shard_map.64), kind=kLoop, calls=%fused_computation | loop fusion | flops 2688 | bytes 16128 | tf_op jit(solution)/shard_map/convert_element_type | solution.py:317
